TPU v7x, 256 devices: a whole 4x4x8 slice. The times are simulated.
256 devices in a mesh: ctx: 8 (over x, y_hi), mp: 32 (over y_lo, z, core).
Axes of the slice: x: 4, y: 4 (y_hi: 2, y_lo: 2; y = y_hi * 2 + y_lo), z: 8, core: 2. Of those that a mesh axis runs over, the one named last changes fastest.
Arguments:
- hidden_states: bfloat16 [24576, 8192], P('ctx', 'mp'), may hold values from -8 to 8
- route_slot: int32 [4608], P('ctx'), may hold values from 0 to 3071, as said below
- route_live: int32 [4608], P('ctx'), may hold values from 0 to 1, as said below
- router_weight: bfloat16 [8192], replicated, may hold values from -0.0625 to 0.0625
- query_weight: bfloat16 [8192, 8192], P(None, 'mp')
- keyval_weight: bfloat16 [8192, 2048], P(None, 'mp')
- output_weight: bfloat16 [8192, 8192], P('mp'), may hold values from -0.75 to 0.75
Outputs:
- mixed_states: bfloat16 [24576, 8192], P('ctx', 'mp')
Inputs may be any that keep to these rules, and one draw needn't show every extreme that they name: `route_slot`: within each owner's 576 slots the live slots come first and hold distinct ascending offsets below 3072; dead slots hold 0. The last token of every owner is routed. `route_live`: each owner has from 192 to 576 live slots, all at its first slots; together they are exactly 3072; some owner has all 576 live.
All inputs are finite; a program needn't handle non-finite values.
Results may differ from a plain program's by a relative error of at most 0.03.
Values may be sent and summed in bfloat16 or wider, within the bound.
No kernel may reach another device: no remote copies, remote signals or barrier semaphores. Data moves between devices by JAX's collectives and lax.ppermute only.
A program may use at most 128 MiB of HBM per device.

v0:
```python
import jax
import jax.numpy as jnp
from jax import lax
from jax.sharding import PartitionSpec as P

GROUP = 8
HQ_DEV = 2
far_position = 1073741824


def partner_2(value, axis, apart):
    return lax.ppermute(value, axis, [(i, i ^ 1 << apart) for i in range(lax.axis_size(axis))])


def attend_block(state_tuple, queries, query_pos, keyval_rows, key_pos):
    running_max, running_sum, weighted = state_tuple
    width = queries.shape[1]
    key_part = keyval_rows[:, :width]
    value_part = keyval_rows[:, width:]
    scores = lax.dot_general(
        queries, key_part, (((1,), (1,)), ((), ())), preferred_element_type=jnp.float32
    ) * width ** (-0.5)
    allowed = key_pos[None, :] <= query_pos[:, None]
    masked = jnp.where(allowed, scores, -1e30)
    new_max = jnp.maximum(running_max, jnp.max(masked, axis=1))
    weights = jnp.where(allowed, jnp.exp(masked - new_max[:, None]), 0.0)
    shrink = jnp.exp(running_max - new_max)
    running_sum = running_sum * shrink + jnp.sum(weights, axis=1)
    weighted = weighted * shrink[:, None] + jnp.dot(
        weights.astype(jnp.bfloat16), value_part, preferred_element_type=jnp.float32
    )
    return (new_max, running_sum, weighted)


def routed_update(
    routed_rows, positions, router_weight, query_weight, keyval_weight, output_weight
):
    row_total = routed_rows.shape[0]
    local_width = query_weight.shape[1]
    head_width = keyval_weight.shape[1] * GROUP // (2 * HQ_DEV)
    head_count = local_width // head_width
    fragment = lax.all_gather(routed_rows, "mp", axis=1, tiled=True)
    keyval_rows = keyval_weight
    query_acc = jnp.dot(fragment, query_weight, preferred_element_type=jnp.float32)
    keyval_acc = jnp.dot(fragment, keyval_rows, preferred_element_type=jnp.float32)
    logit_acc = jnp.dot(fragment, router_weight, preferred_element_type=jnp.float32)
    query_acc, keyval_acc, logit_acc = (query_acc, keyval_acc, logit_acc)
    queries = query_acc.astype(jnp.bfloat16)
    stacked_queries = (
        queries.reshape(row_total, head_count, head_width)
        .transpose(1, 0, 2)
        .reshape(head_count * row_total, head_width)
    )
    stacked_pos = jnp.tile(positions, head_count)
    own_keyval = keyval_acc.astype(jnp.bfloat16)
    mp_index = lax.axis_index("mp")
    bit_count = (GROUP // HQ_DEV).bit_length() - 1
    for bit_number in range(bit_count):
        partner = partner_2(own_keyval, "mp", bit_number)
        upper_side = mp_index >> bit_number & 1 == 1
        own_keyval = jnp.where(
            upper_side,
            jnp.concatenate([partner, own_keyval], axis=1),
            jnp.concatenate([own_keyval, partner], axis=1),
        )
    stacked_rows = head_count * row_total
    start_state = (
        jnp.full((stacked_rows,), -1e30, jnp.float32),
        jnp.zeros((stacked_rows,), jnp.float32),
        jnp.zeros((stacked_rows, head_width), jnp.float32),
    )
    state_tuple = start_state
    keyval_rows = lax.all_gather(own_keyval, "ctx", axis=0, tiled=True)
    key_pos = lax.all_gather(positions, "ctx", axis=0, tiled=True)
    amount = keyval_rows.shape[0]
    blocks = amount // 512

    def step_block(inner, item):
        return (attend_block(inner, stacked_queries, stacked_pos, item[0], item[1]), None)

    stacked = (keyval_rows.reshape(blocks, 512, keyval_rows.shape[1]), key_pos.reshape(blocks, 512))
    state_tuple, unused = lax.scan(step_block, state_tuple, stacked)
    running_max, running_sum, weighted = state_tuple
    stacked_attended = (weighted / running_sum[:, None]).astype(jnp.bfloat16)
    attended = (
        stacked_attended.reshape(head_count, row_total, head_width)
        .transpose(1, 0, 2)
        .reshape(row_total, local_width)
    )
    gate_value = jax.nn.sigmoid(logit_acc)
    combined = lax.psum_scatter(
        lax.dot_general(
            output_weight, attended, (((0,), (1,)), ((), ())), preferred_element_type=jnp.float32
        ).astype(jnp.bfloat16),
        "mp",
        scatter_dimension=0,
        tiled=True,
    ).astype(jnp.float32)
    return (gate_value[:, None] * combined.T).astype(jnp.bfloat16)


def local(
    hidden_states, route_slot, route_live, router_weight, query_weight, keyval_weight, output_weight
):
    seq_dev = hidden_states.shape[0]
    ctx_id = lax.axis_index("ctx")
    own_rows = jnp.take(hidden_states, route_slot, axis=0)
    positions = jnp.where(route_live == 1, ctx_id * seq_dev + route_slot, far_position)
    update = routed_update(
        own_rows, positions, router_weight, query_weight, keyval_weight, output_weight
    )
    addition = jnp.where(route_live[:, None] == 1, update.astype(jnp.float32), 0.0)
    widened = hidden_states.astype(jnp.float32).at[route_slot].add(addition)
    return widened.astype(jnp.bfloat16)


def solution(mesh):
    placed = (P("ctx", "mp"), P("ctx"), P("ctx"), P(), P(None, "mp"), P(None, "mp"), P("mp", None))
    return jax.shard_map(
        local, mesh=mesh, in_specs=placed, out_specs=P("ctx", "mp"), check_vma=False
    )
```

profile of v0, /device:TPU:20, one launch (start us, length us, event | category | flops | bytes accessed | tf_op | source)
XLA Modules:
  0.0 374.4 jit_solution(8200890812531677743)
XLA Ops:
  6.5 0.8 compare_and_fusion
  7.3 1.3 dynamic-slice
  9.2 0.8 fusion.25
  10.1 3.8 %gather_fusion = bf16[576,256]{1,0:T(8,128)(2,1)S(1)} fusion(bf16[3072,256]{1,0:T(8,128)(2,1)} %param.9, s32[1024]{0:T(1024)S(1)} %pad_clamp_fusion), kind=kCustom, calls=%fused_computation | custom fusion | bytes 592128 | tf_op jit(solution)/shard_map/jit(_take)/gather | solution.py:107
  13.9 0.9 broadcast_select_fusion
  14.8 96.4 %all-gather.3.cloned.1.call-done = bf16[576,8192]{1,0:T(8,128)(2,1)} async-done(((bf16[576,256]{1,0:T(8,128)(2,1)}), bf16[576,8192]{1,0:T(8,128)(2,1)}) %all-gather.3.cloned.1.call-update) | async-done | bytes 9437200 | tf_op jit(solution)/shard_map/all_gather | solution.py:42
  111.2 6.6 %convolution_convert_fusion.2 = bf16[576,64]{0,1:T(8,128)(2,1)S(1)} fusion(bf16[576,8192]{1,0:T(8,128)(2,1)} %all-gather.3.cloned.1.call-done, bf16[8192,64]{0,1:T(8,128)(2,1)S(1)} %copy-done), kind=kOutput, calls=%fused_computation.27 | convolution fusion | flops 604016640 | bytes 10559488 | tf_op jit(solution)/shard_map/dot_general | solution.py:45
  118.1 1.0 collective-permute-done
  119.2 2.2 collective-permute-start.1
  121.4 4.6 %collective-permute-done.1 = bf16[576,128]{0,1:T(8,128)(2,1)S(1)} collective-permute-done((bf16[576,128]{0,1:T(8,128)(2,1)S(1)}, bf16[576,128]{0,1:T(8,128)(2,1)S(1)}, u32[]{:S(2)}, u32[]{:S(2)}) %collective-permute-start.1) | collective-permute-done | bytes 147488 | tf_op jit(solution)/shard_map/ppermute | solution.py:12
  126.1 0.9 copy.13
  127.0 34.8 %all-reduce = s32[4608]{0:T(1024)S(1)} all-reduce(s32[4608]{0:T(1024)S(1)} %get-tuple-element.106), channel_id=1, replica_groups=mesh['ctx'=8,'mp'=32] {'ctx'}, use_global_device_ids=true, to_apply=%add | all-reduce | flops 4608 | bytes 36864
  161.8 7.8 %convolution_convert_fusion.1 = bf16[576,256]{1,0:T(8,128)(2,1)S(1)} fusion(bf16[576,8192]{1,0:T(8,128)(2,1)} %all-gather.3.cloned.1.call-done, bf16[8192,256]{1,0:T(8,128)(2,1)} %param.13), kind=kOutput, calls=%fused_computation.26 | convolution fusion | flops 2416066560 | bytes 13926400 | tf_op jit(solution)/shard_map/dot_general | solution.py:44
  169.7 14.9 %all-gather.5.cloned.1.call-done = bf16[4608,256]{1,0:T(8,128)(2,1)} async-done(((bf16[576,256]{1,0:T(8,128)(2,1)}), bf16[4608,256]{1,0:T(8,128)(2,1)}) %all-gather.5.cloned.1.call-update) | async-done | bytes 2359312 | tf_op jit(solution)/shard_map/all_gather | solution.py:73
  184.6 27.0 %while.15 = (s32[]{:T(128)}, f32[1152]{0:T(1024)S(1)}, f32[1152]{0:T(1024)S(1)}, f32[1152,128]{1,0:T(8,128)S(1)}, s32[9,512]{1,0:T(8,128)S(1)}, /*index=5*/bf16[...) while((s32[]{:T(128)}, f32[1152]{0:T(1024)S(1)}, ...), condition=%wide.region_3.4_spmd.clone, body=%wide.region_0.3_spmd.clone.sunk | while | flops 309515904 | bytes 9467265 | solution.py:82
  184.7 1.0 dynamic-slice_bitcast_fusion.2
  185.7 0.5 fusion.44
  186.8 0.8 convolution_add_fusion.2
  187.7 1.0 dynamic-slice_bitcast_fusion.2
  188.7 0.5 fusion.44
  189.8 0.8 convolution_add_fusion.2
  190.8 1.0 dynamic-slice_bitcast_fusion.2
  191.7 0.5 fusion.44
  192.8 0.8 convolution_add_fusion.2
  193.8 1.0 dynamic-slice_bitcast_fusion.2
  194.7 0.5 fusion.44
  195.8 0.8 convolution_add_fusion.2
  196.8 1.0 dynamic-slice_bitcast_fusion.2
  197.7 0.5 fusion.44
  198.8 0.8 convolution_add_fusion.2
  199.8 1.0 dynamic-slice_bitcast_fusion.2
  200.8 0.5 fusion.44
  201.8 0.8 convolution_add_fusion.2
  202.8 1.0 dynamic-slice_bitcast_fusion.2
  203.8 0.5 fusion.44
  204.8 0.8 convolution_add_fusion.2
  205.8 1.0 dynamic-slice_bitcast_fusion.2
  206.8 0.5 fusion.44
  207.8 0.8 convolution_add_fusion.2
  208.8 1.0 dynamic-slice_bitcast_fusion.2
  210.8 0.8 convolution_add_fusion.2
  212.2 7.3 %fusion.15 = bf16[8192,576]{0,1:T(8,128)(2,1)} fusion(bf16[256,8192]{1,0:T(8,128)(2,1)} %param.15, bf16[72,8,2,128]{3,2,1,0:T(2,128)(2,1)S(1)} %bitcast.36), kind=kOutput, calls=%fused_computation.25 | convolution fusion | flops 2420637696 | bytes 13926400 | tf_op jit(solution)/shard_map/dot_general | solution.py:92
  219.5 1.4 copy-done.1
  220.9 1.9 convert_element_type.35
  222.9 6.2 %convolution_reduce_fusion = f32[576]{0:T(1024)S(1)} fusion(bf16[576,8192]{1,0:T(8,128)(2,1)} %all-gather.3.cloned.1.call-done, bf16[8192,1]{0,1:T(2,128)(2,1)S(1)} %reshape.60), kind=kOutput, calls=%fused_computation.28 | convolution fusion | flops 9437184 | bytes 9455872 | tf_op jit(solution)/shard_map/dot_general | solution.py:46
  229.1 124.3 %reduce-scatter.2.cloned.1.call-done = bf16[256,576]{0,1:T(8,128)(2,1)} async-done(((bf16[8192,576]{0,1:T(8,128)(2,1)}), bf16[256,576]{0,1:T(8,128)(2,1)}) %reduce-scatter.2.cloned.1.call-update) | async-done | bytes 294928 | tf_op jit(solution)/shard_map/reduce_scatter | solution.py:91
  353.4 11.3 %scatter_custom_fusion = f32[3072,256]{1,0:T(8,128)} fusion(f32[3072,256]{1,0:T(8,128)} %convert_element_type.35, s32[576]{0:T(1024)S(1)} %get-tuple-element.111, bf16[256,576]{0,1:T(8,128)(2,1)} %reduce-scatter.2.cloned.1.call-done, f32[]{:T(128)} %constant.33.clone.1, f32[576]{0:T(1024)S(1)} %add_divide_fusion, pred[576]{0:T(1024)(128)(4,1)S(1)} %get-tuple-element.108), kind=kCustom, calls=%fused_computation.29 | custom fusion | flops 884736 | bytes 3446272 | tf_op jit(solution)/shard_map/scatter-add | solution.py:113
  364.7 3.2 convert_element_type.44
  (90 shorter events, 7.3 us)
Async XLA Ops:
  6.5 104.7 %copy-start = (bf16[8192,64]{0,1:T(8,128)(2,1)S(1)}, bf16[8192,64]{0,1:T(8,128)(2,1)}, u32[]{:S(2)}) copy-start(bf16[8192,64]{0,1:T(8,128)(2,1)} %param.14) | copy-start | bytes 3145732
  6.5 104.7 %all-gather.3.cloned.1.call-start = ((), (), s32[]{:S(2)}) async-start(), calls=%async_computation.1 | async-start | bytes 9732096 | tf_op jit(solution)/shard_map/all_gather | solution.py:42
  14.7 169.9 %all-gather.5.cloned.1.call-start = ((), (), s32[]{:S(2)}) async-start(), calls=%async_computation.2 | async-start | bytes 2654208 | tf_op jit(solution)/shard_map/all_gather | solution.py:73
  117.8 1.4 collective-permute-start
  119.2 6.8 %collective-permute-start.1 = (bf16[576,128]{0,1:T(8,128)(2,1)S(1)}, bf16[576,128]{0,1:T(8,128)(2,1)S(1)}, u32[]{:S(2)}, u32[]{:S(2)}) collective-permute-start(bf16[576,128]{0,1:T(8,128)(2,1)S(1)} %maximum_select_fusion.1), channel_id=1, source_target_pairs={{0,2},{1,3},{2,0},{3,1},{4,6},{5,7},{6,4},{7,5},{8,10},{9,11},{10,... | collective-permute-start | bytes 442376 | tf_op jit(solution)/shard_map/ppermute | solution.py:12
  127.0 226.5 %reduce-scatter.2.cloned.1.call-start = ((), (), s32[]{:S(2)}) async-start(), calls=%async_computation.3 | async-start | bytes 9732096 | tf_op jit(solution)/shard_map/reduce_scatter | solution.py:91
  219.5 1.4 copy-start.1
  220.9 1.9 copy-start.2
Sparse Core Ops, SparseCore 0:
  14.9 96.2 all-gather.2
  127.1 57.5 all-gather.4
  219.7 133.7 reduce-scatter.1
where the time goes:
time: 375 us; the launch traced here: 374 us
  waiting for transfers between devices  241 us (64%)
  matrix products  40.1 us (11%)
  blocking collectives  34.8 us (9%)
  other arithmetic  23.8 us (6%)
  local copies, waits for them, and re-layouts  17.3 us (5%)
  between operations  13.9 us (4%)
    reduce_scatter x1, waiting for transfers between devices, routed_update(): lax.psum_scatter(lax.dot_general(output_weight, attended, (((0,), (1,)),...  124 us
    all_gather x1, waiting for transfers between devices, routed_update(): fragment = lax.all_gather(routed_rows, 'mp', axis=1, tiled=True)  96.4 us
    unnamed x1, blocking collectives  34.8 us
    all_gather x1, waiting for transfers between devices, routed_update(): keyval_rows = lax.all_gather(own_keyval, 'ctx', axis=0, tiled=True)  14.9 us
    scatter-add x1, other arithmetic, local(): widened = hidden_states.astype(jnp.float32).at[route_slot].add(addition)  11.3 us
    squeeze x9, local copies, waits for them, and re-layouts, routed_update(): state_tuple, unused = lax.scan(step_block, state_tuple, stacked)  8.71 us
    dot_general x1, matrix products, routed_update(): jnp.dot(fragment, query_weight, preferred_element_type=jnp.float32)  7.76 us
    dot_general x9, matrix products, attend_block(): jnp.dot(weights.astype(jnp.bfloat16), value_part, preferred_element_type=...  7.55 us
  transfers between devices with their start and end apart: 5, of which 5 were waited for; matrix products, arithmetic and copies ran while one was open for 4% of the time, Pallas kernels for 0%

commit v1 on v0

--- a/solution.py
+++ b/solution.py
@@ -70,7 +70,8 @@
         jnp.zeros((stacked_rows, head_width), jnp.float32),
     )
     state_tuple = start_state
-    keyval_rows = lax.all_gather(own_keyval, "ctx", axis=0, tiled=True)
+    sent = jnp.stack([own_keyval] * lax.axis_size("ctx"))
+    keyval_rows = jnp.concatenate(lax.all_to_all(sent, "ctx", 0, 0), axis=0)
     key_pos = lax.all_gather(positions, "ctx", axis=0, tiled=True)
     amount = keyval_rows.shape[0]
     blocks = amount // 512

time: 375 us -> 401 us (1.069)
  blocking collectives: 34.8 us -> 57.5 us
  waiting for transfers between devices: 241 us -> 223 us
  matrix products: 40.1 us -> 49.7 us
  starting transfers between devices: 2.59 us -> 9.72 us
    unnamed x1, blocking collectives: 34.8 us -> 57.5 us
    all_gather x1 -> x0, waiting for transfers between devices: 14.9 us -> none  [routed_update(): keyval_rows = lax.all_gather(own_keyval, 'ctx', axis=0, tiled=True)]
    dot_general x9, matrix products: 4.71 us -> 13.9 us  [attend_block(): lax.dot_general(queries, key_part, (((1,), (1,)), ((), ())), preferred_el...]
    squeeze x9, local copies, waits for them, and re-layouts: 8.71 us -> 0.16 us  [routed_update(): state_tuple, unused = lax.scan(step_block, state_tuple, stacked)]
    while x9 -> x45, local copies, waits for them, and re-layouts: 0.02 us -> 7.27 us
    all_to_all x0 -> x1, starting transfers between devices: none -> 7.21 us  [routed_update(): keyval_rows = jnp.concatenate(lax.all_to_all(sent, 'ctx', 0, 0), axis=0)]
  transfers between devices with their start and end apart: 5 -> 5, of which waited for: 5 -> 4; matrix products, arithmetic and copies ran while one was open for 4% -> 5% of each run, Pallas kernels for 0% -> 0%
where the time goes in v1:
time: 401 us; the launch traced here: 400 us
  waiting for transfers between devices  223 us (56%)
  blocking collectives  57.5 us (14%)
  matrix products  49.7 us (12%)
  other arithmetic  24.9 us (6%)
  local copies, waits for them, and re-layouts  20.2 us (5%)
  between operations  14.1 us (4%)
  starting transfers between devices  9.72 us (2%)
    reduce_scatter x1, waiting for transfers between devices, routed_update(): lax.psum_scatter(lax.dot_general(output_weight, attended, (((0,), (1,)),...  121 us
    all_gather x1, waiting for transfers between devices, routed_update(): fragment = lax.all_gather(routed_rows, 'mp', axis=1, tiled=True)  96.4 us
    unnamed x1, blocking collectives  57.5 us
    dot_general x9, matrix products, attend_block(): lax.dot_general(queries, key_part, (((1,), (1,)), ((), ())), preferred_el...  13.9 us
    scatter-add x1, other arithmetic, local(): widened = hidden_states.astype(jnp.float32).at[route_slot].add(addition)  11.3 us
    dot_general x1, matrix products, routed_update(): jnp.dot(fragment, query_weight, preferred_element_type=jnp.float32)  8.18 us
  transfers between devices with their start and end apart: 5, of which 4 were waited for; matrix products, arithmetic and copies ran while one was open for 5% of the time, Pallas kernels for 0%

profile of v1, /device:TPU:20, one launch (start us, length us, event | category | flops | bytes accessed | tf_op | source)
XLA Modules:
  0.0 399.6 jit_solution(13527398318436526223)
XLA Ops:
  7.3 1.3 dynamic-slice
  9.2 0.8 fusion.25
  10.1 3.8 gather_fusion
  13.9 0.9 broadcast_select_fusion
  14.8 96.4 %all-gather.2.cloned.1.call-done = bf16[576,8192]{1,0:T(8,128)(2,1)} async-done(((bf16[576,256]{1,0:T(8,128)(2,1)}), bf16[576,8192]{1,0:T(8,128)(2,1)}) %all-gather.2.cloned.1.call-update) | async-done | bytes 9437200 | tf_op jit(solution)/shard_map/all_gather | solution.py:42
  111.2 6.6 %convolution_convert_fusion.2 = bf16[576,64]{0,1:T(8,128)(2,1)S(1)} fusion(bf16[576,8192]{1,0:T(8,128)(2,1)} %all-gather.2.cloned.1.call-done, bf16[8192,64]{0,1:T(8,128)(2,1)S(1)} %copy-done), kind=kOutput, calls=%fused_computation.27 | convolution fusion | flops 604016640 | bytes 10559488 | tf_op jit(solution)/shard_map/dot_general | solution.py:45
  118.1 1.0 collective-permute-done
  119.2 2.2 collective-permute-start.1
  121.4 4.6 %collective-permute-done.1 = bf16[576,128]{0,1:T(8,128)(2,1)S(1)} collective-permute-done((bf16[576,128]{0,1:T(8,128)(2,1)S(1)}, bf16[576,128]{0,1:T(8,128)(2,1)S(1)}, u32[]{:S(2)}, u32[]{:S(2)}) %collective-permute-start.1) | collective-permute-done | bytes 147488 | tf_op jit(solution)/shard_map/ppermute | solution.py:12
  126.2 1.6 stack.2
  127.8 7.2 %all-to-all-start = ((bf16[8,576,256]{2,1,0:T(8,128)(2,1)}), bf16[8,576,256]{2,1,0:T(8,128)(2,1)S(1)}, u32[]{:S(2)}, u32[]{:S(2)}) async-start(bf16[8,576,256]{2,1,0:T(8,128)(2,1)} %stack.2), calls=%async_computation | async-start | bytes 4718592 | tf_op jit(solution)/shard_map/all_to_all | solution.py:74
  135.0 57.5 %all-reduce = s32[4608]{0:T(1024)S(1)} all-reduce(s32[4608]{0:T(1024)S(1)} %get-tuple-element.98), channel_id=1, replica_groups=mesh['ctx'=8,'mp'=32] {'ctx'}, use_global_device_ids=true, to_apply=%add | all-reduce | flops 4608 | bytes 36864
  192.5 8.2 %convolution_convert_fusion.1 = bf16[576,256]{1,0:T(8,128)(2,1)} fusion(bf16[576,8192]{1,0:T(8,128)(2,1)} %all-gather.2.cloned.1.call-done, bf16[8192,256]{1,0:T(8,128)(2,1)} %param.13), kind=kOutput, calls=%fused_computation.26 | convolution fusion | flops 2416066560 | bytes 13926400 | tf_op jit(solution)/shard_map/dot_general | solution.py:44
  200.6 1.7 reshape.42
  202.4 1.7 copy.11
  204.1 34.9 %while.15 = (s32[]{:T(128)}, f32[1152]{0:T(1024)S(1)}, f32[1152]{0:T(1024)S(1)}, f32[1152,128]{1,0:T(8,128)}, s32[9,512]{1,0:T(8,128)S(1)}, /*index=5*/bf16[9,51...) while((s32[]{:T(128)}, f32[1152]{0:T(1024)S(1)}, ...), condition=%wide.region_3.4_spmd.clone, body=%wide.region_0.3_spmd.clone.sunk | while | flops 309515904 | bytes 14185913 | solution.py:83
  204.2 1.6 fusion.44
  206.3 0.8 convolution_add_fusion.2
  207.2 0.8 copy-done.3
  208.1 1.5 fusion.44
  210.2 0.8 convolution_add_fusion.2
  211.1 0.8 copy-done.3
  212.0 1.5 fusion.44
  214.1 0.8 convolution_add_fusion.2
  215.0 0.8 copy-done.3
  215.9 1.5 fusion.44
  218.0 0.8 convolution_add_fusion.2
  218.8 0.8 copy-done.3
  219.8 1.5 fusion.44
  221.8 0.8 convolution_add_fusion.2
  222.7 0.8 copy-done.3
  223.6 1.6 fusion.44
  225.7 0.8 convolution_add_fusion.2
  226.6 0.8 copy-done.3
  227.5 1.6 fusion.44
  229.6 0.8 convolution_add_fusion.2
  231.4 1.6 fusion.44
  233.5 0.8 convolution_add_fusion.2
  235.3 1.6 fusion.44
  237.4 0.8 convolution_add_fusion.2
  239.0 1.3 divide_convert_fusion
  240.6 7.3 %fusion.15 = bf16[8192,576]{0,1:T(8,128)(2,1)} fusion(bf16[256,8192]{1,0:T(8,128)(2,1)} %param.15, bf16[72,8,2,128]{3,2,1,0:T(2,128)(2,1)S(1)} %bitcast.37), kind=kOutput, calls=%fused_computation.25 | convolution fusion | flops 2420637696 | bytes 13926400 | tf_op jit(solution)/shard_map/dot_general | solution.py:93
  247.9 1.4 copy-done.1
  249.3 1.9 convert_element_type.35
  251.3 6.2 %convolution_reduce_fusion = f32[576]{0:T(1024)S(1)} fusion(bf16[576,8192]{1,0:T(8,128)(2,1)} %all-gather.2.cloned.1.call-done, bf16[8192,1]{0,1:T(2,128)(2,1)S(1)} %reshape.69), kind=kOutput, calls=%fused_computation.28 | convolution fusion | flops 9437184 | bytes 9455872 | tf_op jit(solution)/shard_map/dot_general | solution.py:46
  257.5 120.8 %reduce-scatter.2.cloned.1.call-done = bf16[256,576]{0,1:T(8,128)(2,1)} async-done(((bf16[8192,576]{0,1:T(8,128)(2,1)}), bf16[256,576]{0,1:T(8,128)(2,1)}) %reduce-scatter.2.cloned.1.call-update) | async-done | bytes 294928 | tf_op jit(solution)/shard_map/reduce_scatter | solution.py:92
  378.3 11.3 %scatter_custom_fusion = f32[3072,256]{1,0:T(8,128)} fusion(f32[3072,256]{1,0:T(8,128)} %convert_element_type.35, s32[576]{0:T(1024)S(1)} %get-tuple-element.103, bf16[256,576]{0,1:T(8,128)(2,1)} %reduce-scatter.2.cloned.1.call-done, f32[]{:T(128)} %constant.33.clone.1, f32[576]{0:T(1024)S(1)} %add_divide_fusion, pred[576]{0:T(1024)(128)(4,1)S(1)} %get-tuple-element.100), kind=kCustom, calls=%fused_computation.29 | custom fusion | flops 884736 | bytes 3446272 | tf_op jit(solution)/shard_map/scatter-add | solution.py:114
  389.5 3.2 convert_element_type.44
  (126 shorter events, 9.9 us)
Async XLA Ops:
  6.5 104.7 %copy-start = (bf16[8192,64]{0,1:T(8,128)(2,1)S(1)}, bf16[8192,64]{0,1:T(8,128)(2,1)}, u32[]{:S(2)}) copy-start(bf16[8192,64]{0,1:T(8,128)(2,1)} %param.14) | copy-start | bytes 3145732
  6.5 104.7 %all-gather.2.cloned.1.call-start = ((), (), s32[]{:S(2)}) async-start(), calls=%async_computation.2 | async-start | bytes 9732096 | tf_op jit(solution)/shard_map/all_gather | solution.py:42
  117.8 1.4 collective-permute-start
  119.2 6.8 %collective-permute-start.1 = (bf16[576,128]{0,1:T(8,128)(2,1)S(1)}, bf16[576,128]{0,1:T(8,128)(2,1)S(1)}, u32[]{:S(2)}, u32[]{:S(2)}) collective-permute-start(bf16[576,128]{0,1:T(8,128)(2,1)S(1)} %maximum_select_fusion.1), channel_id=1, source_target_pairs={{0,2},{1,3},{2,0},{3,1},{4,6},{5,7},{6,4},{7,5},{8,10},{9,11},{10,... | collective-permute-start | bytes 442376 | tf_op jit(solution)/shard_map/ppermute | solution.py:12
  127.8 76.3 %all-to-all-start = ((bf16[8,576,256]{2,1,0:T(8,128)(2,1)}), bf16[8,576,256]{2,1,0:T(8,128)(2,1)S(1)}, u32[]{:S(2)}, u32[]{:S(2)}) async-start(bf16[8,576,256]{2,1,0:T(8,128)(2,1)} %stack.2), calls=%async_computation | async-start | bytes 4718592 | tf_op jit(solution)/shard_map/all_to_all | solution.py:74
  135.0 243.3 %reduce-scatter.2.cloned.1.call-start = ((), (), s32[]{:S(2)}) async-start(), calls=%async_computation.3 | async-start | bytes 9732096 | tf_op jit(solution)/shard_map/reduce_scatter | solution.py:92
  204.2 2.1 copy-start.2
  207.2 0.8 copy-start.3
  208.1 2.1 copy-start.2
  211.1 0.8 copy-start.3
  212.0 2.1 copy-start.2
  214.9 0.8 copy-start.3
  215.9 2.1 copy-start.2
  218.8 0.8 copy-start.3
  219.7 2.1 copy-start.2
  222.7 0.8 copy-start.3
  223.6 2.1 copy-start.2
  226.6 0.8 copy-start.3
  227.5 2.1 copy-start.2
  230.5 0.8 copy-start.3
  231.4 2.1 copy-start.2
  234.3 0.8 copy-start.3
  235.3 2.1 copy-start.2
  238.2 0.8 copy-start.3
  247.9 1.4 copy-start.1
  249.3 1.9 copy-start.4
Sparse Core Ops, SparseCore 0:
  14.9 96.2 all-gather.1
  248.0 130.2 reduce-scatter.1
